TPU v7x, 256 devices: a whole 4x4x8 slice. The times are simulated.
256 devices in a mesh: narrow: 16 (over z, core), wide: 16 (over x, y).
Axes of the slice: x: 4, y: 4, z: 8, core: 2. Of those that a mesh axis runs over, the one named last changes fastest.
Arguments:
- inputs: bfloat16 [2048, 8192], P('narrow', 'wide'), may hold values from -6 to 6
- gate_blocks: bfloat16 [112, 16, 128, 128], P('wide', 'narrow'), may hold values from -0.125 to 0.125
- up_blocks: bfloat16 [112, 16, 128, 128], P('wide', 'narrow'), may hold values from -0.125 to 0.125
- pattern: int32 [112, 16], P('wide'), may hold values from 0 to 63, as said below
- grad_hidden: bfloat16 [2048, 14336], P('narrow', 'wide'), may hold values from -0.59765625 to 0.59765625
Outputs:
- hidden: bfloat16 [2048, 14336], P('narrow', 'wide')
- grad_inputs: bfloat16 [2048, 8192], P('narrow', 'wide')
- grad_gate: bfloat16 [112, 16, 128, 128], P('wide', 'narrow')
- grad_up: bfloat16 [112, 16, 128, 128], P('wide', 'narrow')
Inputs may be any that keep to these rules, and one draw needn't show every extreme that they name: pattern[j, k] = b_j XOR m_k, with one offset b_j for each block column and 16 distinct masks m_k common to all block columns, so each block column lists 16 distinct block rows.
All inputs are finite; a program needn't handle non-finite values.
Results may differ from a plain program's by a relative error of at most 0.023.
Values may be sent and summed in bfloat16 or wider, within the bound.
A program may use at most 128 MiB of HBM per device.

v0:
```python
import jax
import jax.numpy as jnp
from jax import lax
from jax.sharding import PartitionSpec as P


def silu_parts(gate_sum):
    sigmoid_value = jax.nn.sigmoid(gate_sum)
    return (gate_sum * sigmoid_value, sigmoid_value * (1.0 + gate_sum * (1.0 - sigmoid_value)))


def shards(inputs, gate_blocks, up_blocks, pattern, grad_hidden):
    tokens_here = inputs.shape[0]
    block_size = gate_blocks.shape[2]
    columns = gate_blocks.shape[0]
    full_inputs = lax.all_gather(inputs, "wide", axis=1, tiled=True)
    row_blocks = full_inputs.shape[1] // block_size
    input_blocks = full_inputs.reshape(tokens_here, row_blocks, block_size)

    def picks_for():
        return jnp.take(input_blocks, pattern, axis=1)

    gate_all, up_all = (
        lax.all_gather(gate_blocks, "narrow", axis=1, tiled=True),
        lax.all_gather(up_blocks, "narrow", axis=1, tiled=True),
    )
    pieces = (gate_all, up_all)
    picked = picks_for()
    gate_sum = jnp.einsum("tjkb,jkbc->tjc", picked, pieces[0], preferred_element_type=jnp.float32)
    up_sum = jnp.einsum("tjkb,jkbc->tjc", picked, pieces[1], preferred_element_type=jnp.float32)
    gate_sum, up_sum = (gate_sum, up_sum)
    activation, derivative = silu_parts(gate_sum)
    hidden = (activation * up_sum).astype(jnp.bfloat16)
    cotangent = grad_hidden.reshape(tokens_here, columns, block_size).astype(jnp.float32)
    d_gate = (cotangent * up_sum * derivative).astype(jnp.bfloat16)
    d_up = (cotangent * activation).astype(jnp.bfloat16)
    zero_inputs = jnp.zeros((tokens_here, row_blocks, block_size), jnp.float32)
    pieces = (gate_all, up_all)
    number_slots = pieces[0].shape[1]

    def one_slot(k, running):
        gate_slot = lax.dynamic_index_in_dim(pieces[0], k, 1, keepdims=False)
        up_slot = lax.dynamic_index_in_dim(pieces[1], k, 1, keepdims=False)
        contribution = jnp.einsum(
            "tjc,jbc->tjb", d_gate, gate_slot, preferred_element_type=jnp.float32
        )
        contribution = contribution + jnp.einsum(
            "tjc,jbc->tjb", d_up, up_slot, preferred_element_type=jnp.float32
        )
        targets = lax.dynamic_index_in_dim(pattern, k, 1, keepdims=False)
        return running.at[:, targets].add(contribution)

    partial_inputs = lax.fori_loop(0, number_slots, one_slot, zero_inputs)
    grad_inputs = lax.psum_scatter(
        partial_inputs.reshape(tokens_here, row_blocks * block_size).astype(jnp.bfloat16),
        "wide",
        scatter_dimension=1,
        tiled=True,
    )
    picked_all = picks_for()
    gate_terms = jnp.einsum(
        "tjkb,tjc->jkbc", picked_all, d_gate, preferred_element_type=jnp.float32
    )
    up_terms = jnp.einsum("tjkb,tjc->jkbc", picked_all, d_up, preferred_element_type=jnp.float32)
    grad_gate, grad_up = (
        lax.psum_scatter(
            gate_terms.astype(jnp.bfloat16), "narrow", scatter_dimension=1, tiled=True
        ).astype(jnp.float32),
        lax.psum_scatter(
            up_terms.astype(jnp.bfloat16), "narrow", scatter_dimension=1, tiled=True
        ).astype(jnp.float32),
    )
    return (
        hidden.reshape(tokens_here, columns * block_size),
        grad_inputs,
        grad_gate.astype(jnp.bfloat16),
        grad_up.astype(jnp.bfloat16),
    )


def solution(mesh):
    placed = (
        P("narrow", "wide"),
        P("wide", "narrow", None, None),
        P("wide", "narrow", None, None),
        P("wide", None),
        P("narrow", "wide"),
    )
    return jax.shard_map(
        shards,
        mesh=mesh,
        in_specs=placed,
        out_specs=(
            P("narrow", "wide"),
            P("narrow", "wide"),
            P("wide", "narrow", None, None),
            P("wide", "narrow", None, None),
        ),
        check_vma=False,
    )
```

profile of v0, /device:TPU:32, one launch (start us, length us, event | category | flops | bytes accessed | tf_op | source)
XLA Modules:
  0.0 384.9 jit_solution(9591232748475014344)
XLA Ops:
  7.2 1.7 copy.60
  8.9 1.8 copy.65
  10.8 1.8 copy.63
  16.0 47.6 %all-gather.4.cloned.1.call-done = bf16[128,8192]{0,1:T(8,128)(2,1)} async-done(((bf16[128,512]{0,1:T(8,128)(2,1)}), bf16[128,8192]{0,1:T(8,128)(2,1)}) %all-gather.4.cloned.1.call-update) | async-done | bytes 2097168 | tf_op jit(solution)/shard_map/all_gather | solution.py:16
  63.6 3.2 copy.61
  66.8 3.0 gather_fusion
  69.8 6.1 %copy.62 = bf16[7,16,128,128]{2,3,1,0:T(8,128)(2,1)} copy(bf16[7,16,128,128]{3,2,1,0:T(8,128)(2,1)} %bitcast.89) | data formatting | bytes 7340032 | tf_op jit(solution)/shard_map/jit(_take)/gather | solution.py:21
  75.9 31.0 %all-gather.8.cloned.1.call-done = bf16[7,16,128,128]{2,3,1,0:T(8,128)(2,1)} async-done(((bf16[7,1,128,128]{2,3,1,0:T(8,128)(2,1)}), bf16[7,16,128,128]{2,3,1,0:T(8,128)(2,1)}) %all-gather.8.cloned.1.call-update) | async-done | bytes 3670032 | tf_op jit(solution)/shard_map/all_gather | solution.py:25
  106.9 4.4 %fusion.27 = f32[128,7,128]{0,2,1:T(8,128)S(1)} fusion(bf16[7,16,128,128]{2,3,1,0:T(8,128)(2,1)} %all-gather.8.cloned.1.call-done, bf16[7,16,128,128]{2,3,1,0:T(8,128)(2,1)} %copy.62, pred[7,16]{1,0:T(8,128)(4,1)S(1)} %compare_and_fusion), kind=kOutput, calls=%fused_computation.31 | convolution fusion | flops 471597056 | bytes 7798896 | tf_op jit(solution)/shard_map/tjkb,jkbc->tjc/dot_general | solution.py:30
  111.3 38.3 %all-gather.6.cloned.1.call-done = bf16[7,16,128,128]{2,3,1,0:T(8,128)(2,1)} async-done(((bf16[7,1,128,128]{2,3,1,0:T(8,128)(2,1)}), bf16[7,16,128,128]{2,3,1,0:T(8,128)(2,1)}) %all-gather.6.cloned.1.call-update) | async-done | bytes 3670032 | tf_op jit(solution)/shard_map/all_gather | solution.py:24
  149.6 4.5 %multiply_convert_fusion = (bf16[128,7,128]{0,2,1:T(8,128)(2,1)S(1)}, bf16[128,7,128]{0,2,1:T(8,128)(2,1)S(1)}, bf16[128,7,128]{0,2,1:T(8,128)(2,1)S(1)}) fusion(f32[128,7,128]{0,2,1:T(8,128)S(1)} %bitcast.91, f32[128,7,128]{0,2,1:T(8,128)S(1)} %fusion.27, bf16[7,16,128,128]{2,3,1,0:T(8,128)(2,1)} %all-gather.6.cloned.1.call-done, ...), kind=kOutput, calls=%fused_computation.33 | convolution fusion | flops 473317376 | bytes 8945776 | tf_op jit(solution)/shard_map/tjkb,jkbc->tjc/dot_general | solution.py:29
  154.3 5.1 %fusion.17 = bf16[7,16,128,128]{3,2,1,0:T(8,128)(2,1)} fusion(bf16[7,16,128,128]{2,3,1,0:T(8,128)(2,1)} %copy.62, pred[7,16]{1,0:T(8,128)(4,1)S(1)} %compare_and_fusion, bf16[128,7,128]{0,2,1:T(8,128)(2,1)S(1)} %get-tuple-element.191), kind=kOutput, calls=%fused_computation.23 | convolution fusion | flops 473432064 | bytes 7569520 | tf_op jit(solution)/shard_map/tjkb,tjc->jkbc/dot_general | solution.py:61
  159.6 5.0 %fusion.20 = bf16[7,16,128,128]{3,2,1,0:T(8,128)(2,1)} fusion(bf16[7,16,128,128]{2,3,1,0:T(8,128)(2,1)} %copy.62, pred[7,16]{1,0:T(8,128)(4,1)S(1)} %compare_and_fusion, bf16[128,7,128]{0,2,1:T(8,128)(2,1)S(1)} %get-tuple-element.190), kind=kOutput, calls=%fused_computation.24 | convolution fusion | flops 473432064 | bytes 7569520 | tf_op jit(solution)/shard_map/tjkb,tjc->jkbc/dot_general | solution.py:64
  164.7 2.5 broadcast_in_dim.15
  167.1 86.0 %while.13 = (s32[]{:T(128)}, f32[128,64,128]{2,0,1:T(8,128)}, s32[7,16]{0,1:T(8,128)S(1)}, bf16[7,16,128,128]{2,3,1,0:T(8,128)(2,1)}, bf16[128,7,128]{2,0,1:T(8,...) while((s32[]{:T(128)}, f32[128,64,128]{2,0,1:T(8,128)}, ...), condition=%wide.region_2.4_spmd, body=%wide.region_0.3_spmd.sunk | while | flops 58949656 | bytes 4587709 | solution.py:53
  169.9 2.6 scatter_fusion
  173.7 1.3 fusion.57
  175.2 2.7 scatter_fusion
  180.6 2.7 scatter_fusion
  184.5 1.3 fusion.57
  186.0 2.7 scatter_fusion
  189.9 1.3 fusion.57
  191.4 2.7 scatter_fusion
  195.3 1.3 fusion.57
  196.8 2.7 scatter_fusion
  199.4 1.3 fusion.56
  200.7 1.3 fusion.57
  202.1 2.7 scatter_fusion
  206.1 1.3 fusion.57
  207.5 2.7 scatter_fusion
  211.4 1.3 fusion.57
  212.9 2.6 scatter_fusion
  218.3 2.6 scatter_fusion
  222.2 1.3 fusion.57
  223.6 2.6 scatter_fusion
  227.5 1.3 fusion.57
  229.0 2.6 scatter_fusion
  234.3 2.6 scatter_fusion
  239.7 2.7 scatter_fusion
  242.4 1.3 fusion.56
  243.6 1.3 fusion.57
  245.1 2.7 scatter_fusion
  249.0 1.3 fusion.57
  250.5 2.7 scatter_fusion
  253.1 3.9 %copy_bitcast_fusion = bf16[128,8192]{1,0:T(8,128)(2,1)} fusion(f32[128,64,128]{2,0,1:T(8,128)} %get-tuple-element.129), kind=kLoop, calls=%fused_computation.25 | loop fusion | flops 1048576 | bytes 6291456 | tf_op jit(solution)/shard_map/convert_element_type | solution.py:55
  258.5 34.1 %all-reduce.5.cloned.1.call-done = (bf16[7,16,128,128]{3,2,1,0:T(8,128)(2,1)}, bf16[7,16,128,128]{3,2,1,0:T(8,128)(2,1)}) async-done(((bf16[7,16,128,128]{3,2,1,0:T(8,128)(2,1)}, bf16[7,16,128,128]{3,2,1,0:T(8,128)(2,1)}), (bf16[7,16,128,128]{3,2,1,0:T(8,128)(2,1)}, bf16[7,16,128,128]{3,2,1,0:T(8,128)(2,1)})) %all-reduce.5.cloned.1.call-update) | async-done | bytes 7340048
  292.6 2.5 constant_dynamic-slice_fusion.1
  295.1 83.3 %reduce-scatter.8.cloned.1.call-done = bf16[128,512]{1,0:T(8,128)(2,1)} async-done(((bf16[128,8192]{1,0:T(8,128)(2,1)}), bf16[128,512]{1,0:T(8,128)(2,1)}) %reduce-scatter.8.cloned.1.call-update) | async-done | bytes 131088 | tf_op jit(solution)/shard_map/reduce_scatter | solution.py:54
  (73 shorter events, 32.4 us)
Async XLA Ops:
  7.2 56.4 %all-gather.4.cloned.1.call-start = ((), (), s32[]{:S(2)}) async-start(), calls=%async_computation.1 | async-start | bytes 2228224 | tf_op jit(solution)/shard_map/all_gather | solution.py:16
  8.9 98.0 %all-gather.8.cloned.1.call-start = ((), (), s32[]{:S(2)}) async-start(), calls=%async_computation.3 | async-start | bytes 3899392 | tf_op jit(solution)/shard_map/all_gather | solution.py:25
  10.7 138.8 %all-gather.6.cloned.1.call-start = ((), (), s32[]{:S(2)}) async-start(), calls=%async_computation.2 | async-start | bytes 3899392 | tf_op jit(solution)/shard_map/all_gather | solution.py:24
  12.6 280.0 %all-reduce.5.cloned.1.call-start = ((), (), s32[]{:S(2)}) async-start(), calls=%async_computation.5 | async-start | bytes 14680064
  164.6 213.7 %reduce-scatter.8.cloned.1.call-start = ((), (), s32[]{:S(2)}) async-start(), calls=%async_computation.4 | async-start | bytes 2228224 | tf_op jit(solution)/shard_map/reduce_scatter | solution.py:54
  253.1 3.9 %copy-start = (u32[256]{0:T(256)S(1)}, u32[256]{0:T(256)}, u32[]{:S(2)}) copy-start(u32[256]{0:T(256)} %constant.58) | copy-start | bytes 3076
Sparse Core Ops, SparseCore 0:
  11.0 52.5 all-gather.3
  66.0 40.8 all-gather.7
  109.3 40.2 all-gather.5
  164.7 127.8 all-reduce.4
  296.6 81.7 reduce-scatter.7
where the time goes:
time: 387 us; the launch traced here: 385 us
  waiting for transfers between devices  234 us (60%)
  matrix products  59.2 us (15%)
  other arithmetic  47.8 us (12%)
  local copies, waits for them, and re-layouts  29.3 us (8%)
  between operations  13.8 us (4%)
    reduce_scatter x1, waiting for transfers between devices, shards(): lax.psum_scatter(partial_inputs.reshape(tokens_here, row_blocks * block_s...  83.3 us
    all_gather x1, waiting for transfers between devices, shards(): full_inputs = lax.all_gather(inputs, 'wide', axis=1, tiled=True)  47.6 us
    scatter-add x16, other arithmetic, one_slot(): return running.at[:, targets].add(contribution)  42.4 us
    all_gather x1, waiting for transfers between devices, shards(): lax.all_gather(gate_blocks, 'narrow', axis=1, tiled=True)  38.3 us
    unnamed x6, waiting for transfers between devices  34.2 us
    all_gather x1, waiting for transfers between devices, shards(): lax.all_gather(up_blocks, 'narrow', axis=1, tiled=True)  31 us
    dot_general x16, matrix products, one_slot(): jnp.einsum('tjc,jbc->tjb', d_up, up_slot, preferred_element_type=jnp.floa...  20.2 us
    dot_general x16, matrix products, one_slot(): jnp.einsum('tjc,jbc->tjb', d_gate, gate_slot, preferred_element_type=jnp....  20 us
  transfers between devices with their start and end apart: 5, of which 5 were waited for; matrix products, arithmetic and copies ran while one was open for 31% of the time, Pallas kernels for 0%

commit v1 on v0

--- a/solution.py
+++ b/solution.py
@@ -13,7 +13,9 @@
     tokens_here = inputs.shape[0]
     block_size = gate_blocks.shape[2]
     columns = gate_blocks.shape[0]
-    full_inputs = lax.all_gather(inputs, "wide", axis=1, tiled=True)
+    full_inputs = jnp.concatenate(
+        lax.all_to_all(jnp.stack([inputs] * lax.axis_size("wide")), "wide", 0, 0), axis=1
+    )
     row_blocks = full_inputs.shape[1] // block_size
     input_blocks = full_inputs.reshape(tokens_here, row_blocks, block_size)
 

time: 387 us -> 335 us (0.87)
  waiting for transfers between devices: 234 us -> 175 us
  starting transfers between devices: 0.21 us -> 7.2 us
    all_gather x1 -> x0, waiting for transfers between devices: 47.6 us -> none  [shards(): full_inputs = lax.all_gather(inputs, 'wide', axis=1, tiled=True)]
    all_gather x1, waiting for transfers between devices: 31 us -> 0.01 us  [shards(): lax.all_gather(up_blocks, 'narrow', axis=1, tiled=True)]
    all_to_all x0 -> x1, waiting for transfers between devices: none -> 30 us  [shards(): lax.all_to_all(jnp.stack([inputs] * lax.axis_size('wide')), 'wide', 0, 0)]
    all_gather x1, waiting for transfers between devices: 38.3 us -> 27.9 us  [shards(): lax.all_gather(gate_blocks, 'narrow', axis=1, tiled=True)]
    all_to_all x0 -> x1, starting transfers between devices: none -> 7.03 us  [shards(): lax.all_to_all(jnp.stack([inputs] * lax.axis_size('wide')), 'wide', 0, 0)]
    another operation x0 -> x2, local copies, waits for them, and re-layouts: none -> 4.97 us  [the longest x1 3.22 us: shards(): input_blocks = full_inputs.reshape(tokens_here, row_blocks, block_size)]
    unnamed x8 -> x14, local copies, waits for them, and re-layouts: 9.13 us -> 9.9 us
    unnamed x6 -> x5, waiting for transfers between devices: 34.2 us -> 34.1 us
  transfers between devices with their start and end apart: 5 -> 5, of which waited for: 5 -> 4; matrix products, arithmetic and copies ran while one was open for 31% -> 35% of each run, Pallas kernels for 0% -> 0%
where the time goes in v1:
time: 335 us; the launch traced here: 333 us
  waiting for transfers between devices  175 us (52%)
  matrix products  59.4 us (18%)
  other arithmetic  46.5 us (14%)
  local copies, waits for them, and re-layouts  30.2 us (9%)
  between operations  13.9 us (4%)
  starting transfers between devices  7.2 us (2%)
    reduce_scatter x1, waiting for transfers between devices, shards(): lax.psum_scatter(partial_inputs.reshape(tokens_here, row_blocks * block_s...  83.3 us
    scatter-add x16, other arithmetic, one_slot(): return running.at[:, targets].add(contribution)  42.5 us
    unnamed x5, waiting for transfers between devices  34.1 us
    all_to_all x1, waiting for transfers between devices, shards(): lax.all_to_all(jnp.stack([inputs] * lax.axis_size('wide')), 'wide', 0, 0)  30 us
    all_gather x1, waiting for transfers between devices, shards(): lax.all_gather(gate_blocks, 'narrow', axis=1, tiled=True)  27.9 us
    dot_general x16, matrix products, one_slot(): jnp.einsum('tjc,jbc->tjb', d_up, up_slot, preferred_element_type=jnp.floa...  20.2 us
    dot_general x16, matrix products, one_slot(): jnp.einsum('tjc,jbc->tjb', d_gate, gate_slot, preferred_element_type=jnp....  20 us
    unnamed x14, local copies, waits for them, and re-layouts  9.9 us
  transfers between devices with their start and end apart: 5, of which 4 were waited for; matrix products, arithmetic and copies ran while one was open for 35% of the time, Pallas kernels for 0%

profile of v1, /device:TPU:32, one launch (start us, length us, event | category | flops | bytes accessed | tf_op | source)
XLA Modules:
  0.0 332.5 jit_solution(6360533235871033290)
XLA Ops:
  7.2 1.8 copy.48
  9.1 1.8 copy.46
  11.9 1.8 stack.2
  13.7 7.0 %all-to-all-start = ((bf16[16,128,512]{1,2,0:T(8,128)(2,1)}), bf16[16,128,512]{1,2,0:T(8,128)(2,1)S(1)}, u32[]{:S(2)}, u32[]{:S(2)}) async-start(bf16[16,128,512]{1,2,0:T(8,128)(2,1)} %stack.2), calls=%async_computation | async-start | bytes 4194304 | tf_op jit(solution)/shard_map/all_to_all | solution.py:17
  21.1 30.0 %all-to-all-done = bf16[16,128,512]{1,2,0:T(8,128)(2,1)S(1)} async-done(((bf16[16,128,512]{1,2,0:T(8,128)(2,1)}), bf16[16,128,512]{1,2,0:T(8,128)(2,1)S(1)}, u32[]{:S(2)}, u32[]{:S(2)}) %all-to-all-start) | async-done | bytes 2097184 | tf_op jit(solution)/shard_map/all_to_all | solution.py:17
  51.1 1.3 copy-done
  52.5 3.2 copy.44
  55.7 2.9 gather_fusion
  58.6 6.1 %copy.45 = bf16[7,16,128,128]{2,3,1,0:T(8,128)(2,1)} copy(bf16[7,16,128,128]{3,2,1,0:T(8,128)(2,1)} %bitcast.91) | data formatting | bytes 7340032 | tf_op jit(solution)/shard_map/jit(_take)/gather | solution.py:23
  64.8 4.5 %fusion.27 = f32[128,7,128]{0,2,1:T(8,128)S(1)} fusion(bf16[7,16,128,128]{2,3,1,0:T(8,128)(2,1)} %all-gather.5.cloned.1.call-done, bf16[7,16,128,128]{2,3,1,0:T(8,128)(2,1)} %copy.45, pred[7,16]{1,0:T(8,128)(4,1)S(1)} %compare_and_fusion), kind=kOutput, calls=%fused_computation.31 | convolution fusion | flops 471597056 | bytes 7798896 | tf_op jit(solution)/shard_map/tjkb,jkbc->tjc/dot_general | solution.py:32
  69.3 27.9 %all-gather.3.cloned.1.call-done = bf16[7,16,128,128]{2,3,1,0:T(8,128)(2,1)} async-done(((bf16[7,1,128,128]{2,3,1,0:T(8,128)(2,1)}), bf16[7,16,128,128]{2,3,1,0:T(8,128)(2,1)}) %all-gather.3.cloned.1.call-update) | async-done | bytes 3670032 | tf_op jit(solution)/shard_map/all_gather | solution.py:26
  97.2 4.6 %multiply_convert_fusion = (bf16[128,7,128]{0,2,1:T(8,128)(2,1)S(1)}, bf16[128,7,128]{0,2,1:T(8,128)(2,1)S(1)}, bf16[128,7,128]{0,2,1:T(8,128)(2,1)S(1)}) fusion(f32[128,7,128]{0,2,1:T(8,128)S(1)} %bitcast.93, f32[128,7,128]{0,2,1:T(8,128)S(1)} %fusion.27, bf16[7,16,128,128]{2,3,1,0:T(8,128)(2,1)} %all-gather.3.cloned.1.call-done, ...), kind=kOutput, calls=%fused_computation.33 | convolution fusion | flops 473317376 | bytes 8945776 | tf_op jit(solution)/shard_map/tjkb,jkbc->tjc/dot_general | solution.py:31
  101.9 5.1 %fusion.17 = bf16[7,16,128,128]{3,2,1,0:T(8,128)(2,1)} fusion(bf16[7,16,128,128]{2,3,1,0:T(8,128)(2,1)} %copy.45, pred[7,16]{1,0:T(8,128)(4,1)S(1)} %compare_and_fusion, bf16[128,7,128]{0,2,1:T(8,128)(2,1)S(1)} %get-tuple-element.180), kind=kOutput, calls=%fused_computation.23 | convolution fusion | flops 473432064 | bytes 7569520 | tf_op jit(solution)/shard_map/tjkb,tjc->jkbc/dot_general | solution.py:63
  107.2 5.0 %fusion.20 = bf16[7,16,128,128]{3,2,1,0:T(8,128)(2,1)} fusion(bf16[7,16,128,128]{2,3,1,0:T(8,128)(2,1)} %copy.45, pred[7,16]{1,0:T(8,128)(4,1)S(1)} %compare_and_fusion, bf16[128,7,128]{0,2,1:T(8,128)(2,1)S(1)} %get-tuple-element.179), kind=kOutput, calls=%fused_computation.24 | convolution fusion | flops 473432064 | bytes 7569520 | tf_op jit(solution)/shard_map/tjkb,tjc->jkbc/dot_general | solution.py:66
  112.3 2.5 broadcast_in_dim.15
  114.7 86.1 %while.13 = (s32[]{:T(128)}, f32[128,64,128]{2,0,1:T(8,128)}, s32[7,16]{0,1:T(8,128)S(1)}, bf16[7,16,128,128]{2,3,1,0:T(8,128)(2,1)}, bf16[128,7,128]{2,0,1:T(8,...) while((s32[]{:T(128)}, f32[128,64,128]{2,0,1:T(8,128)}, ...), condition=%wide.region_2.4_spmd, body=%wide.region_0.3_spmd.sunk | while | flops 58949656 | bytes 4587709 | solution.py:55
  117.4 2.6 scatter_fusion
  121.3 1.3 fusion.57
  122.8 2.7 scatter_fusion
  128.2 2.7 scatter_fusion
  132.1 1.3 fusion.57
  133.6 2.7 scatter_fusion
  137.5 1.3 fusion.57
  139.0 2.7 scatter_fusion
  144.4 2.7 scatter_fusion
  148.3 1.3 fusion.57
  149.8 2.6 scatter_fusion
  153.7 1.3 fusion.57
  155.1 2.7 scatter_fusion
  159.1 1.3 fusion.57
  160.5 2.7 scatter_fusion
  165.9 2.6 scatter_fusion
  168.5 1.3 fusion.56
  169.8 1.3 fusion.57
  171.3 2.6 scatter_fusion
  175.2 1.3 fusion.57
  176.6 2.6 scatter_fusion
  182.0 2.6 scatter_fusion
  187.3 2.7 scatter_fusion
  190.0 1.3 fusion.56
  191.3 1.3 fusion.57
  192.7 2.7 scatter_fusion
  196.7 1.3 fusion.57
  198.2 2.6 scatter_fusion
  200.8 3.9 %copy_bitcast_fusion = bf16[128,8192]{1,0:T(8,128)(2,1)} fusion(f32[128,64,128]{2,0,1:T(8,128)} %get-tuple-element.129), kind=kLoop, calls=%fused_computation.25 | loop fusion | flops 1048576 | bytes 6291456 | tf_op jit(solution)/shard_map/convert_element_type | solution.py:57
  206.2 34.0 %all-reduce.5.cloned.1.call-done = (bf16[7,16,128,128]{3,2,1,0:T(8,128)(2,1)}, bf16[7,16,128,128]{3,2,1,0:T(8,128)(2,1)}) async-done(((bf16[7,16,128,128]{3,2,1,0:T(8,128)(2,1)}, bf16[7,16,128,128]{3,2,1,0:T(8,128)(2,1)}), (bf16[7,16,128,128]{3,2,1,0:T(8,128)(2,1)}, bf16[7,16,128,128]{3,2,1,0:T(8,128)(2,1)})) %all-reduce.5.cloned.1.call-update) | async-done | bytes 7340048
  240.2 2.5 constant_dynamic-slice_fusion.1
  242.7 83.3 %reduce-scatter.8.cloned.1.call-done = bf16[128,512]{1,0:T(8,128)(2,1)} async-done(((bf16[128,8192]{1,0:T(8,128)(2,1)}), bf16[128,512]{1,0:T(8,128)(2,1)}) %reduce-scatter.8.cloned.1.call-update) | async-done | bytes 131088 | tf_op jit(solution)/shard_map/reduce_scatter | solution.py:56
  (79 shorter events, 31.7 us)
Async XLA Ops:
  7.2 57.6 %all-gather.5.cloned.1.call-start = ((), (), s32[]{:S(2)}) async-start(), calls=%async_computation.3 | async-start | bytes 3899392 | tf_op jit(solution)/shard_map/all_gather | solution.py:27
  9.0 11.8 %copy-start.1 = (bf16[128,896]{1,0:T(8,128)(2,1)S(1)}, bf16[128,896]{1,0:T(8,128)(2,1)}, u32[]{:S(2)}) copy-start(bf16[128,896]{1,0:T(8,128)(2,1)} %param.13) | copy-start | bytes 688132
  9.0 88.2 %all-gather.3.cloned.1.call-start = ((), (), s32[]{:S(2)}) async-start(), calls=%async_computation.2 | async-start | bytes 3899392 | tf_op jit(solution)/shard_map/all_gather | solution.py:26
  10.9 10.0 %copy-start.2 = (s32[7,16]{1,0:T(8,128)S(1)}, s32[7,16]{1,0:T(8,128)}, u32[]{:S(2)}) copy-start(s32[7,16]{1,0:T(8,128)} %param.12) | copy-start | bytes 1348
  13.7 37.4 %all-to-all-start = ((bf16[16,128,512]{1,2,0:T(8,128)(2,1)}), bf16[16,128,512]{1,2,0:T(8,128)(2,1)S(1)}, u32[]{:S(2)}, u32[]{:S(2)}) async-start(bf16[16,128,512]{1,2,0:T(8,128)(2,1)} %stack.2), calls=%async_computation | async-start | bytes 4194304 | tf_op jit(solution)/shard_map/all_to_all | solution.py:17
  20.7 219.5 %all-reduce.5.cloned.1.call-start = ((), (), s32[]{:S(2)}) async-start(), calls=%async_computation.5 | async-start | bytes 14680064
  51.1 1.3 copy-start
  112.2 213.8 %reduce-scatter.8.cloned.1.call-start = ((), (), s32[]{:S(2)}) async-start(), calls=%async_computation.4 | async-start | bytes 2228224 | tf_op jit(solution)/shard_map/reduce_scatter | solution.py:56
  200.8 3.9 %copy-start.3 = (u32[256]{0:T(256)S(1)}, u32[256]{0:T(256)}, u32[]{:S(2)}) copy-start(u32[256]{0:T(256)} %constant.58) | copy-start | bytes 3076
Sparse Core Ops, SparseCore 0:
  10.4 44.0 all-gather.4
  56.9 40.2 all-gather.2
  112.3 127.8 all-reduce.4
  244.2 81.7 reduce-scatter.7
